TPU v7x, 256 devices: a whole 4x4x8 slice. The times are simulated.
256 devices in a mesh: row: 16 (over y, x), col: 8 (over z_lo, core), band: 2 (over z_hi).
Axes of the slice: x: 4, y: 4, z: 8 (z_hi: 2, z_lo: 4; z = z_hi * 4 + z_lo), core: 2. Of those that a mesh axis runs over, the one named last changes fastest.
Arguments:
- panel: bfloat16 [32, 512, 512], P('row', ('col', 'band')), may hold values from -6 to 6
- inverse: bfloat16 [2, 512, 512], replicated, may hold values from -0.25 to 0.25
- trail_grad: bfloat16 [32, 32, 512, 512], P('row', ('col', 'band')), may hold values from -0.046875 to 0.046875
- factor_grad: bfloat16 [32, 512, 512], P('row', ('col', 'band')), may hold values from -6 to 6
- present: int32 [32, 32], P('row', ('col', 'band')), may hold values from 0 to 1, as said below
- supernode: int32 [32], replicated, may hold values from 0 to 1
Outputs:
- panel_adjoint: bfloat16 [32, 512, 512], P('row', ('col', 'band'))
- inverse_adjoint: float32 [2, 512, 512], replicated
Inputs may be any that keep to these rules, and one draw needn't show every extreme that they name: Every diagonal tile is present; rows differ widely in how many tiles are present.
All inputs are finite; a program needn't handle non-finite values.
Results may differ from a plain program's by a relative error of at most 0.0055.
Values may be sent and summed in bfloat16 or wider, within the bound.
A program may use at most 64 MiB of HBM per device.

v0:
```python
import jax
import jax.numpy as jnp
from jax import lax
from jax.sharding import PartitionSpec as P


def from_root(value, axis, source):
    kept = jnp.where(lax.axis_index(axis) == source, value, 0).astype(value.dtype)
    return lax.psum(kept, axis)


def pick_inverse(inverse, labels):
    first = inverse[0][None, :, :]
    second = inverse[1][None, :, :]
    return jnp.where((labels == 0)[:, None, None], first, second)


def local(panel, inverse, trail_grad, factor_grad, present, supernode):
    rows_here = trail_grad.shape[0]
    cols_here = trail_grad.shape[1]
    tile = trail_grad.shape[2]
    total_rows = rows_here * lax.axis_size("row")
    row_index = lax.axis_index("row")
    col_index = lax.axis_index(("col", "band"))
    row_labels = lax.dynamic_slice_in_dim(supernode, row_index * rows_here, rows_here)
    col_labels = lax.dynamic_slice_in_dim(supernode, col_index * cols_here, cols_here)
    root = col_index * cols_here // rows_here
    row_inverse = pick_inverse(inverse, row_labels)
    factor_piece = jnp.einsum(
        "iab,ibc->iac", panel, row_inverse, preferred_element_type=jnp.float32
    ).astype(jnp.bfloat16)
    factor_row = lax.all_gather(factor_piece, ("col", "band"), axis=1, tiled=True)
    factor_block = from_root(factor_row, "row", root)
    weight = present * (row_labels[:, None] == col_labels[None, :]).astype(jnp.int32)
    masked = trail_grad * weight.astype(jnp.bfloat16)[:, :, None, None]
    mirror_part = jnp.einsum(
        "ijab,iae->jbe", masked, factor_row, preferred_element_type=jnp.float32
    )
    mirror = lax.psum(mirror_part, "row")
    mirror_cols = jnp.transpose(mirror, (1, 0, 2))
    is_owner = (row_index == root).astype(jnp.float32)
    placed = mirror_cols
    placed = placed * is_owner
    direct = jnp.einsum("ijab,jbe->aie", masked, factor_block, preferred_element_type=jnp.float32)
    summed = lax.psum_scatter(direct + placed, ("col", "band"), scatter_dimension=0, tiled=True)
    factor_total = (jnp.transpose(factor_grad.astype(jnp.float32), (1, 0, 2)) - summed).astype(
        jnp.bfloat16
    )
    panel_adjoint = jnp.einsum(
        "aie,ife->iaf", factor_total, row_inverse, preferred_element_type=jnp.float32
    ).astype(jnp.bfloat16)
    onehot = (row_labels[:, None] == jnp.arange(2, dtype=jnp.int32)[None, :]).astype(jnp.float32)
    terms = jnp.einsum("iaf,aie->ife", panel, factor_total, preferred_element_type=jnp.float32)
    local_grad = jnp.einsum("is,ife->sfe", onehot, terms)
    inverse_adjoint = lax.psum(local_grad, ("row", "col", "band")) / jnp.sqrt(
        jnp.float32(total_rows * tile)
    )
    return (panel_adjoint, inverse_adjoint)


def solution(mesh):
    in_specs = (
        P("row", ("col", "band"), None),
        P(),
        P("row", ("col", "band"), None, None),
        P("row", ("col", "band"), None),
        P("row", ("col", "band")),
        P(),
    )
    out_specs = (P("row", ("col", "band"), None), P())
    return jax.shard_map(local, mesh=mesh, in_specs=in_specs, out_specs=out_specs, check_vma=False)
```

profile of v0, /device:TPU:2, one launch (start us, length us, event | category | flops | bytes accessed | tf_op | source)
XLA Modules:
  0.0 711.1 jit_solution(867655354191725240)
XLA Ops:
  7.2 0.0 copy-start
  7.2 0.0 copy-start.4
  7.2 0.0 all-gather.2.cloned.1.call-start
  7.2 1.3 slice_bitcast_fusion.1
  8.5 0.0 copy-done.4
  8.5 0.1 broadcast_compare_fusion
  8.6 0.0 copy-done
  8.6 0.0 copy-start.3
  8.6 1.1 fusion.19
  9.7 0.0 all-gather.2.cloned.1.call-update
  9.7 0.0 all-reduce.6.cloned.1.call-start
  9.8 92.1 %all-gather.2.cloned.1.call-done = bf16[2,512,512]{2,1,0:T(8,128)(2,1)} async-done(((bf16[2,32,512]{2,1,0:T(8,128)(2,1)}), bf16[2,512,512]{2,1,0:T(8,128)(2,1)}) %all-gather.2.cloned.1.call-update) | async-done | bytes 1048592 | tf_op jit(solution)/shard_map/all_gather | solution.py:32
  101.9 0.0 copy-start.1
  101.9 1.1 broadcast_select_fusion
  103.0 0.0 all-reduce.6.cloned.1.call-update
  103.0 0.0 all-reduce.8.cloned.1.call-start
  103.1 0.1 dynamic_slice.7
  103.2 0.0 copy-done.3
  103.2 0.1 fusion.36
  103.2 0.3 copy-done.1
  103.5 4.2 fusion.4
  107.8 0.0 all-reduce.8.cloned.1.call-update
  107.8 0.0 all-reduce.12.cloned.1.call-start
  107.8 96.2 %all-reduce.6.cloned.1.call-done = bf16[2,512,512]{2,1,0:T(8,128)(2,1)} async-done(((bf16[2,512,512]{2,1,0:T(8,128)(2,1)}), bf16[2,512,512]{2,1,0:T(8,128)(2,1)}) %all-reduce.6.cloned.1.call-update) | async-done | bytes 1048592 | tf_op jit(solution)/shard_map/psum | solution.py:9
  204.0 104.7 %all-reduce.8.cloned.1.call-done = f32[2,512,512]{1,2,0:T(8,128)} async-done(((f32[2,512,512]{1,2,0:T(8,128)}), f32[2,512,512]{1,2,0:T(8,128)}) %all-reduce.8.cloned.1.call-update) | async-done | bytes 2097168 | tf_op jit(solution)/shard_map/psum | solution.py:39
  308.8 3.9 bitcast_add_fusion
  312.7 2.4 copy.26
  315.1 0.0 copy-start.5
  315.1 0.0 copy-start.2
  315.1 0.0 all-reduce.12.cloned.1.call-update
  315.1 0.0 all-reduce.10.cloned.1.call-start
  315.2 0.6 copy-done.5
  315.8 0.6 dynamic-slice
  317.0 113.6 %all-reduce.12.cloned.1.call-done = f32[512,2,512]{2,1,0:T(2,128)} async-done(((f32[512,2,512]{2,1,0:T(2,128)}), f32[512,2,512]{2,1,0:T(2,128)}) %all-reduce.12.cloned.1.call-update) | async-done | bytes 2097168
  430.6 0.9 constant_dynamic-slice_fusion
  431.6 0.0 copy-done.2
  431.6 0.5 convolution_bitcast_fusion
  432.1 1.0 copy.29
  433.1 2.8 fusion.33
  435.9 0.0 all-reduce.10.cloned.1.call-update
  435.9 1.1 fusion.16
  437.0 263.4 %all-reduce.10.cloned.1.call-done = f32[2,512,512]{2,0,1:T(2,128)} async-done(((f32[2,512,512]{2,0,1:T(2,128)}), f32[2,512,512]{2,0,1:T(2,128)}) %all-reduce.10.cloned.1.call-update) | async-done | bytes 2097168 | tf_op jit(solution)/shard_map/psum | solution.py:55
  700.4 2.5 broadcast_multiply_fusion
  702.9 1.7 copy.30
Async XLA Ops:
  7.2 1.4 copy-start
  7.2 1.3 copy-start.4
  7.2 94.7 %all-gather.2.cloned.1.call-start = ((), (), s32[]{:S(2)}) async-start(), calls=%async_computation | async-start | bytes 1114112 | tf_op jit(solution)/shard_map/all_gather | solution.py:32
  8.6 94.6 %copy-start.3 = (s32[2,2]{1,0:T(2,128)S(1)}, s32[2,2]{1,0:T(2,128)}, u32[]{:S(2)}) copy-start(s32[2,2]{1,0:T(2,128)} %param.10) | copy-start | bytes 52
  9.7 194.3 %all-reduce.6.cloned.1.call-start = ((), (), s32[]{:S(2)}) async-start(), calls=%async_computation.1 | async-start | bytes 2097152 | tf_op jit(solution)/shard_map/psum | solution.py:9
  101.9 1.6 copy-start.1
  103.0 205.7 %all-reduce.8.cloned.1.call-start = ((), (), s32[]{:S(2)}) async-start(), calls=%async_computation.2 | async-start | bytes 4194304 | tf_op jit(solution)/shard_map/psum | solution.py:39
  107.8 322.9 %all-reduce.12.cloned.1.call-start = ((), (), s32[]{:S(2)}) async-start(), calls=%async_computation.4 | async-start | bytes 4194304
  315.1 0.7 copy-start.5
  315.1 116.5 %copy-start.2 = (bf16[2,32,512]{2,1,0:T(8,128)(2,1)S(1)}, bf16[2,32,512]{2,1,0:T(8,128)(2,1)}, u32[]{:S(2)}) copy-start(bf16[2,32,512]{2,1,0:T(8,128)(2,1)} %param.9) | copy-start | bytes 196612
  315.1 385.3 %all-reduce.10.cloned.1.call-start = ((), (), s32[]{:S(2)}) async-start(), calls=%async_computation.3 | async-start | bytes 4194304 | tf_op jit(solution)/shard_map/psum | solution.py:55
Sparse Core Ops, SparseCore 0:
  10.4 91.5 all-gather.1
  105.2 98.8 all-reduce.5
  207.9 100.7 all-reduce.7
  315.3 115.3 all-reduce.11
  436.4 263.9 all-reduce.9
where the time goes:
time: 711 us
  waiting for transfers between devices  670 us (94%)
  between operations  14.5 us (2%)
  matrix products  13.7 us (2%)
  local copies, waits for them, and re-layouts  8.87 us (1%)
    psum x1, waiting for transfers between devices, local(): lax.psum(local_grad, ('row', 'col', 'band'))  263 us
    unnamed x6, waiting for transfers between devices  114 us
    psum x1, waiting for transfers between devices, local(): mirror = lax.psum(mirror_part, 'row')  105 us
    psum x1, waiting for transfers between devices, from_root(): return lax.psum(kept, axis)  96.2 us
    all_gather x1, waiting for transfers between devices, local(): lax.all_gather(factor_piece, ('col', 'band'), axis=1, tiled=True)  92.1 us
  transfers between devices with their start and end apart: 5, of which 5 were waited for; matrix products, arithmetic and copies ran while one was open for 1% of the time, Pallas kernels for 0%

commit v1 on v0

--- a/solution.py
+++ b/solution.py
@@ -36,7 +36,7 @@
     mirror_part = jnp.einsum(
         "ijab,iae->jbe", masked, factor_row, preferred_element_type=jnp.float32
     )
-    mirror = lax.psum(mirror_part, "row")
+    mirror = lax.all_gather(mirror_part, "row").sum(axis=0)
     mirror_cols = jnp.transpose(mirror, (1, 0, 2))
     is_owner = (row_index == root).astype(jnp.float32)
     placed = mirror_cols

time: 711 us -> 813 us (1.14)
  waiting for transfers between devices: 670 us -> 756 us
  other arithmetic: 3.72 us -> 16.5 us
    all_gather x0 -> x1, waiting for transfers between devices: none -> 202 us  [local(): mirror = lax.all_gather(mirror_part, 'row').sum(axis=0)]
    psum x1 -> x0, waiting for transfers between devices: 105 us -> none  [local(): mirror = lax.psum(mirror_part, 'row')]
    reduce_sum x0 -> x1, other arithmetic: none -> 12.7 us  [local(): mirror = lax.all_gather(mirror_part, 'row').sum(axis=0)]
    psum x1, waiting for transfers between devices: 96.2 us -> 85.4 us  [from_root(): return lax.psum(kept, axis)]
  transfers between devices with their start and end apart: 5 -> 5, of which waited for: 5 -> 5; matrix products, arithmetic and copies ran while one was open for 1% -> 2% of each run, Pallas kernels for 0% -> 0%
where the time goes in v1:
time: 813 us; the launch traced here: 812 us
  waiting for transfers between devices  756 us (93%)
  other arithmetic  16.5 us (2%)
  between operations  14.6 us (2%)
  matrix products  13.3 us (2%)
  local copies, waits for them, and re-layouts  11.7 us (1%)
    psum x1, waiting for transfers between devices, local(): lax.psum(local_grad, ('row', 'col', 'band'))  263 us
    all_gather x1, waiting for transfers between devices, local(): mirror = lax.all_gather(mirror_part, 'row').sum(axis=0)  202 us
    unnamed x6, waiting for transfers between devices  114 us
    all_gather x1, waiting for transfers between devices, local(): lax.all_gather(factor_piece, ('col', 'band'), axis=1, tiled=True)  91.9 us
    psum x1, waiting for transfers between devices, from_root(): return lax.psum(kept, axis)  85.4 us
  transfers between devices with their start and end apart: 5, of which 5 were waited for; matrix products, arithmetic and copies ran while one was open for 2% of the time, Pallas kernels for 0%

profile of v1, /device:TPU:2, one launch (start us, length us, event | category | flops | bytes accessed | tf_op | source)
XLA Modules:
  0.0 812.4 jit_solution(15020717351046019355)
XLA Ops:
  7.2 0.0 copy-start
  7.2 0.0 copy-start.4
  7.2 0.0 copy-start.3
  7.2 0.0 copy-start.5
  7.2 0.0 all-gather.4.cloned.1.call-start
  7.3 1.4 slice_bitcast_fusion.1
  8.7 0.0 copy-done.4
  8.7 0.1 broadcast_compare_fusion
  8.8 0.0 copy-done
  8.8 1.1 fusion.19
  9.9 0.0 all-gather.4.cloned.1.call-update
  9.9 0.0 all-gather.6.cloned.1.call-start
  9.9 0.1 dynamic_slice.7
  10.0 0.0 copy-done.3
  10.0 0.1 fusion.36
  10.1 91.9 %all-gather.4.cloned.1.call-done = bf16[2,512,512]{2,1,0:T(8,128)(2,1)} async-done(((bf16[2,32,512]{2,1,0:T(8,128)(2,1)}), bf16[2,512,512]{2,1,0:T(8,128)(2,1)}) %all-gather.4.cloned.1.call-update) | async-done | bytes 1048592 | tf_op jit(solution)/shard_map/all_gather | solution.py:32
  101.9 0.0 copy-done.5
  102.0 3.9 fusion.4
  105.8 0.0 copy-start.1
  105.8 0.0 all-gather.6.cloned.1.call-update
  105.9 0.0 all-reduce.5.cloned.1.call-start
  105.9 1.1 copy-done.1
  107.1 1.1 broadcast_select_fusion
  108.1 0.0 all-reduce.5.cloned.1.call-update
  108.2 0.0 all-reduce.9.cloned.1.call-start
  108.2 201.7 %all-gather.6.cloned.1.call-done = f32[32,512,512]{2,1,0:T(8,128)} async-done(((f32[2,512,512]{2,1,0:T(8,128)}), f32[32,512,512]{2,1,0:T(8,128)}) %all-gather.6.cloned.1.call-update) | async-done | bytes 33554448 | tf_op jit(solution)/shard_map/all_gather | solution.py:39
  309.9 12.7 %reduce_sum.9 = f32[2,512,512]{2,1,0:T(8,128)S(1)} reduce(f32[16,2,512,512]{3,2,1,0:T(8,128)} %bitcast.39, f32[]{:T(128)} %constant.38.clone.1), dimensions={0}, to_apply=%region_1.2 | reduce | flops 7864320 | bytes 35651588 | tf_op jit(solution)/shard_map/reduce_sum | solution.py:39
  322.7 1.8 copy.24
  324.5 85.4 %all-reduce.5.cloned.1.call-done = bf16[2,512,512]{2,1,0:T(8,128)(2,1)} async-done(((bf16[2,512,512]{2,1,0:T(8,128)(2,1)}), bf16[2,512,512]{2,1,0:T(8,128)(2,1)}) %all-reduce.5.cloned.1.call-update) | async-done | bytes 1048592 | tf_op jit(solution)/shard_map/psum | solution.py:9
  409.9 3.9 bitcast_add_fusion
  413.8 2.4 copy.25
  416.3 0.0 copy-start.6
  416.3 0.0 copy-start.2
  416.3 0.0 all-reduce.9.cloned.1.call-update
  416.3 0.0 all-reduce.7.cloned.1.call-start
  416.3 0.6 copy-done.6
  416.9 0.6 dynamic-slice
  418.2 113.8 %all-reduce.9.cloned.1.call-done = f32[512,2,512]{2,1,0:T(2,128)} async-done(((f32[512,2,512]{2,1,0:T(2,128)}), f32[512,2,512]{2,1,0:T(2,128)}) %all-reduce.9.cloned.1.call-update) | async-done | bytes 2097168
  532.0 0.9 constant_dynamic-slice_fusion
  532.9 0.0 copy-done.2
  532.9 0.5 convolution_bitcast_fusion
  533.4 1.0 copy.28
  534.4 2.8 fusion.33
  537.2 0.0 all-reduce.7.cloned.1.call-update
  537.2 1.1 fusion.16
  538.4 263.4 %all-reduce.7.cloned.1.call-done = f32[2,512,512]{2,0,1:T(2,128)} async-done(((f32[2,512,512]{2,0,1:T(2,128)}), f32[2,512,512]{2,0,1:T(2,128)}) %all-reduce.7.cloned.1.call-update) | async-done | bytes 2097168 | tf_op jit(solution)/shard_map/psum | solution.py:55
  801.7 2.5 broadcast_multiply_fusion
  804.2 1.7 copy.29
Async XLA Ops:
  7.2 1.6 copy-start
  7.2 1.5 copy-start.4
  7.2 2.8 copy-start.3
  7.2 94.8 %copy-start.5 = (bf16[2,2,512,512]{3,2,1,0:T(8,128)(2,1)S(1)}, bf16[2,2,512,512]{3,2,1,0:T(8,128)(2,1)}, u32[]{:S(2)}) copy-start(bf16[2,2,512,512]{3,2,1,0:T(8,128)(2,1)} %param.8) | copy-start | bytes 6291460
  7.2 94.7 %all-gather.4.cloned.1.call-start = ((), (), s32[]{:S(2)}) async-start(), calls=%async_computation | async-start | bytes 1114112 | tf_op jit(solution)/shard_map/all_gather | solution.py:32
  9.9 300.1 %all-gather.6.cloned.1.call-start = ((), (), s32[]{:S(2)}) async-start(), calls=%async_computation.3 | async-start | bytes 35651584 | tf_op jit(solution)/shard_map/all_gather | solution.py:39
  105.8 1.2 copy-start.1
  105.9 304.0 %all-reduce.5.cloned.1.call-start = ((), (), s32[]{:S(2)}) async-start(), calls=%async_computation.1 | async-start | bytes 2097152 | tf_op jit(solution)/shard_map/psum | solution.py:9
  108.2 423.8 %all-reduce.9.cloned.1.call-start = ((), (), s32[]{:S(2)}) async-start(), calls=%async_computation.4 | async-start | bytes 4194304
  416.3 0.7 copy-start.6
  416.3 116.6 %copy-start.2 = (bf16[2,32,512]{2,1,0:T(8,128)(2,1)S(1)}, bf16[2,32,512]{2,1,0:T(8,128)(2,1)}, u32[]{:S(2)}) copy-start(bf16[2,32,512]{2,1,0:T(8,128)(2,1)} %param.9) | copy-start | bytes 196612
  416.3 385.4 %all-reduce.7.cloned.1.call-start = ((), (), s32[]{:S(2)}) async-start(), calls=%async_computation.2 | async-start | bytes 4194304 | tf_op jit(solution)/shard_map/psum | solution.py:55
Sparse Core Ops, SparseCore 0:
  10.4 91.5 all-gather.3
  106.0 203.9 all-gather.5
  313.2 96.6 all-reduce.4
  416.4 115.5 all-reduce.8
  537.8 263.9 all-reduce.6

commit v2 on v0

--- a/solution.py
+++ b/solution.py
@@ -2,6 +2,16 @@
 import jax.numpy as jnp
 from jax import lax
 from jax.sharding import PartitionSpec as P
+
+change_goods = lambda vec, across: jnp.concatenate(
+    lax.all_to_all(
+        jnp.stack([vec for _ in range(lax.axis_size(across))], axis=0),
+        axis_name=across,
+        split_axis=0,
+        concat_axis=0,
+    ),
+    1,
+)
 
 
 def from_root(value, axis, source):
@@ -29,7 +39,7 @@
     factor_piece = jnp.einsum(
         "iab,ibc->iac", panel, row_inverse, preferred_element_type=jnp.float32
     ).astype(jnp.bfloat16)
-    factor_row = lax.all_gather(factor_piece, ("col", "band"), axis=1, tiled=True)
+    factor_row = change_goods(factor_piece, ("col", "band"))
     factor_block = from_root(factor_row, "row", root)
     weight = present * (row_labels[:, None] == col_labels[None, :]).astype(jnp.int32)
     masked = trail_grad * weight.astype(jnp.bfloat16)[:, :, None, None]

time: 711 us -> 651 us (0.916)
  waiting for transfers between devices: 670 us -> 600 us
  starting transfers between devices: 0.21 us -> 8.74 us
    all_gather x1 -> x0, waiting for transfers between devices: 92.1 us -> none  [local(): lax.all_gather(factor_piece, ('col', 'band'), axis=1, tiled=True)]
    all_to_all x0 -> x1, waiting for transfers between devices: none -> 28.8 us  [lax.all_to_all(jnp.stack([vec for _ in range(lax.axis_size(across))], axi...]
    all_to_all x0 -> x1, starting transfers between devices: none -> 8.57 us  [lax.all_to_all(jnp.stack([vec for _ in range(lax.axis_size(across))], axi...]
    unnamed x6 -> x5, waiting for transfers between devices: 114 us -> 114 us
where the time goes in v2:
time: 651 us; the launch traced here: 650 us
  waiting for transfers between devices  600 us (92%)
  between operations  14.6 us (2%)
  matrix products  13 us (2%)
  local copies, waits for them, and re-layouts  10.3 us (2%)
  starting transfers between devices  8.74 us (1%)
    psum x1, waiting for transfers between devices, local(): lax.psum(local_grad, ('row', 'col', 'band'))  263 us
    unnamed x5, waiting for transfers between devices  114 us
    psum x1, waiting for transfers between devices, local(): mirror = lax.psum(mirror_part, 'row')  105 us
    psum x1, waiting for transfers between devices, from_root(): return lax.psum(kept, axis)  89.5 us
    all_to_all x1, waiting for transfers between devices, lax.all_to_all(jnp.stack([vec for _ in range(lax.axis_size(across))], axi...  28.8 us
  transfers between devices with their start and end apart: 5, of which 5 were waited for; matrix products, arithmetic and copies ran while one was open for 1% of the time, Pallas kernels for 0%

profile of v2, /device:TPU:2, one launch (start us, length us, event | category | flops | bytes accessed | tf_op | source)
XLA Modules:
  0.0 650.5 jit_solution(14550433136138831093)
XLA Ops:
  7.2 0.0 copy-start
  7.2 0.0 copy-start.3
  7.2 1.3 slice_bitcast_fusion.1
  8.5 0.0 copy-done.3
  8.5 0.1 broadcast_compare_fusion
  8.6 0.0 copy-done
  8.6 0.4 fusion.19
  9.0 1.1 stack.2
  10.1 8.6 %all-to-all-start = ((bf16[16,2,32,512]{3,2,1,0:T(8,128)(2,1)}), bf16[16,2,32,512]{3,2,1,0:T(8,128)(2,1)S(1)}, u32[]{:S(2)}, u32[]{:S(2)}) async-start(bf16[16,2,32,512]{3,2,1,0:T(8,128)(2,1)} %stack.2), calls=%async_computation | async-start | bytes 2097152 | tf_op jit(solution)/shard_map/all_to_all | solution.py:7
  18.7 0.0 all-reduce.6.cloned.1.call-start
  18.8 28.8 %all-to-all-done = bf16[16,2,32,512]{3,2,1,0:T(8,128)(2,1)S(1)} async-done(((bf16[16,2,32,512]{3,2,1,0:T(8,128)(2,1)}), bf16[16,2,32,512]{3,2,1,0:T(8,128)(2,1)S(1)}, u32[]{:S(2)}, u32[]{:S(2)}) %all-to-all-start) | async-done | bytes 1048608 | tf_op jit(solution)/shard_map/all_to_all | solution.py:7
  47.6 0.1 copy.34
  47.7 0.5 copy.35
  48.2 0.0 copy-start.2
  48.3 1.1 broadcast_select_fusion
  49.3 0.0 all-reduce.6.cloned.1.call-update
  49.3 0.0 all-reduce.8.cloned.1.call-start
  49.4 0.1 dynamic_slice.7
  49.5 0.0 copy-done.2
  49.5 0.1 fusion.35
  49.6 4.2 fusion.4
  53.8 0.0 all-reduce.8.cloned.1.call-update
  53.8 0.0 all-reduce.12.cloned.1.call-start
  53.9 89.5 %all-reduce.6.cloned.1.call-done = bf16[2,512,512]{1,2,0:T(8,128)(2,1)} async-done(((bf16[2,512,512]{1,2,0:T(8,128)(2,1)}), bf16[2,512,512]{1,2,0:T(8,128)(2,1)}) %all-reduce.6.cloned.1.call-update) | async-done | bytes 1048592 | tf_op jit(solution)/shard_map/psum | solution.py:19
  143.4 104.7 %all-reduce.8.cloned.1.call-done = f32[2,512,512]{1,2,0:T(8,128)} async-done(((f32[2,512,512]{1,2,0:T(8,128)}), f32[2,512,512]{1,2,0:T(8,128)}) %all-reduce.8.cloned.1.call-update) | async-done | bytes 2097168 | tf_op jit(solution)/shard_map/psum | solution.py:49
  248.1 3.9 bitcast_add_fusion
  252.0 2.4 copy.38
  254.4 0.0 copy-start.4
  254.4 0.0 copy-start.1
  254.4 0.0 all-reduce.12.cloned.1.call-update
  254.4 0.0 all-reduce.10.cloned.1.call-start
  254.5 0.6 copy-done.4
  255.1 0.6 dynamic-slice
  256.3 113.6 %all-reduce.12.cloned.1.call-done = f32[512,2,512]{2,1,0:T(2,128)} async-done(((f32[512,2,512]{2,1,0:T(2,128)}), f32[512,2,512]{2,1,0:T(2,128)}) %all-reduce.12.cloned.1.call-update) | async-done | bytes 2097168
  370.0 0.9 constant_dynamic-slice_fusion
  370.9 0.0 copy-done.1
  370.9 0.5 convolution_bitcast_fusion
  371.4 1.0 copy.41
  372.4 2.8 fusion.32
  375.2 0.0 all-reduce.10.cloned.1.call-update
  375.2 1.1 fusion.16
  376.3 263.4 %all-reduce.10.cloned.1.call-done = f32[2,512,512]{2,0,1:T(2,128)} async-done(((f32[2,512,512]{2,0,1:T(2,128)}), f32[2,512,512]{2,0,1:T(2,128)}) %all-reduce.10.cloned.1.call-update) | async-done | bytes 2097168 | tf_op jit(solution)/shard_map/psum | solution.py:65
  639.7 2.5 broadcast_multiply_fusion
  642.2 1.7 copy.42
Async XLA Ops:
  7.2 1.4 copy-start
  7.2 1.3 copy-start.3
  10.1 37.4 %all-to-all-start = ((bf16[16,2,32,512]{3,2,1,0:T(8,128)(2,1)}), bf16[16,2,32,512]{3,2,1,0:T(8,128)(2,1)S(1)}, u32[]{:S(2)}, u32[]{:S(2)}) async-start(bf16[16,2,32,512]{3,2,1,0:T(8,128)(2,1)} %stack.2), calls=%async_computation | async-start | bytes 2097152 | tf_op jit(solution)/shard_map/all_to_all | solution.py:7
  18.7 124.7 %all-reduce.6.cloned.1.call-start = ((), (), s32[]{:S(2)}) async-start(), calls=%async_computation.1 | async-start | bytes 2097152 | tf_op jit(solution)/shard_map/psum | solution.py:19
  48.2 1.2 copy-start.2
  49.3 198.7 %all-reduce.8.cloned.1.call-start = ((), (), s32[]{:S(2)}) async-start(), calls=%async_computation.2 | async-start | bytes 4194304 | tf_op jit(solution)/shard_map/psum | solution.py:49
  53.8 316.2 %all-reduce.12.cloned.1.call-start = ((), (), s32[]{:S(2)}) async-start(), calls=%async_computation.4 | async-start | bytes 4194304
  254.4 0.7 copy-start.4
  254.4 116.5 %copy-start.1 = (bf16[2,32,512]{2,1,0:T(8,128)(2,1)S(1)}, bf16[2,32,512]{2,1,0:T(8,128)(2,1)}, u32[]{:S(2)}) copy-start(bf16[2,32,512]{2,1,0:T(8,128)(2,1)} %param.9) | copy-start | bytes 196612
  254.4 385.3 %all-reduce.10.cloned.1.call-start = ((), (), s32[]{:S(2)}) async-start(), calls=%async_computation.3 | async-start | bytes 4194304 | tf_op jit(solution)/shard_map/psum | solution.py:65
Sparse Core Ops, SparseCore 0:
  49.5 93.8 all-reduce.5
  147.3 100.7 all-reduce.7
  254.6 115.3 all-reduce.11
  375.8 263.9 all-reduce.9
